TPU v7x, 128 devices: a whole 4x4x4 slice. The times are simulated.
128 devices in a mesh: rep: 8 (over z_lo, x), tp: 16 (over y, z_hi, core).
Axes of the slice: x: 4, y: 4, z: 4 (z_hi: 2, z_lo: 2; z = z_hi * 2 + z_lo), core: 2. Of those that a mesh axis runs over, the one named last changes fastest.
Arguments:
- batch_rows: bfloat16 [12288, 4096], P(('rep', 'tp')), may hold values from -6 to 6
- token_slots: int32 [8, 384], P('rep'), may hold values from 0 to 1535, as said below
- holder_map: int32 [8, 16], P('rep'), may hold values from -2 to 111, as said below
- copies: bfloat16 [32768, 16384], P('rep', 'tp'), may hold values from -6 to 6
- upstream: bfloat16 [3072, 16384], P('rep', 'tp'), may hold values from -18 to 18
- up_act: bfloat16 [3072, 16384], P('rep', 'tp'), may hold values from -6 to 6
- master: float32 [4096, 14336], P('rep', 'tp'), may hold values from -0.078125 to 0.078125
- moment1: bfloat16 [4096, 14336], P('rep', 'tp'), may hold values from -0.75 to 0.75
- moment2: bfloat16 [4096, 14336], P('rep', 'tp'), may hold values from 0.049804688 to 2
Outputs:
- master_next: float32 [4096, 14336], P('rep', 'tp')
- moment1_next: bfloat16 [4096, 14336], P('rep', 'tp')
- moment2_next: bfloat16 [4096, 14336], P('rep', 'tp')
- copy_next: bfloat16 [32768, 16384], P('rep', 'tp')
Inputs may be any that keep to these rules, and one draw needn't show every extreme that they name: `token_slots`: row r lists 384 distinct rows of replica r's batch. `holder_map`: each row is one replica. A row is either -1 everywhere, or holds -2 at exactly 2 devices and at every other device a distinct piece 7 * j + s (0 <= s < 7) with j one of that row's -2 devices, each such piece exactly once. 4 rows are of the second kind. Columns of copies, upstream and up_act that the steps do not name are not read.
All inputs are finite; a program needn't handle non-finite values.
Results may differ from a plain program's by a relative error of at most 0.02.
Values may be sent and summed in bfloat16 or wider, within the bound.
A program may use at most 128 MiB of HBM per device.

v0:
```python
import math
import jax
import jax.numpy as jnp
from jax import lax
from jax.sharding import PartitionSpec as P

beta_one = 0.9
beta_two = 0.95
bias_one = 1.0 - 0.9**10
bias_two = 1.0 - 0.95**10
learn_rate = 0.05
weight_decay = 0.1
epsilon = 1e-08


def from_everyone(array, axis):
    copies = jnp.broadcast_to(array, (lax.axis_size(axis), *array.shape))
    return lax.all_to_all(copies, axis, split_axis=0, concat_axis=0, tiled=True)


def joined_along(pieces, dim):
    shape = list(pieces.shape[1:])
    shape[dim] *= pieces.shape[0]
    return jnp.moveaxis(pieces, 0, dim).reshape(shape)


def gathered_copies(array, axis, dim):
    pieces = from_everyone(array, axis)
    return joined_along(pieces, dim)


def rows_for(lines, count):
    spare = -lines.shape[0] % count
    if not spare:
        return lines
    return jnp.concatenate([lines, jnp.zeros((spare, *lines.shape[1:]), lines.dtype)])


def sum_in_two_steps(array, axis):
    lines = array.reshape(-1, *array.shape[1:][-1:])
    own = lax.psum_scatter(
        rows_for(lines, lax.axis_size(axis)), axis, scatter_dimension=0, tiled=True
    )
    whole = lax.all_gather(own, axis).reshape(-1, *lines.shape[1:])
    return lax.slice_in_dim(whole, 0, len(lines)).reshape(array.shape)


def on_device(
    batch_rows, token_slots, holder_map, copies, upstream, up_act, master, moment1, moment2
):
    tp_count = lax.axis_size("tp")
    position = lax.axis_index("tp")
    chosen = token_slots[0]
    whole_batch = lax.all_gather(batch_rows, "tp", axis=0, tiled=True)
    inputs = jnp.take(whole_batch, chosen, axis=0)
    holders = holder_map[0]
    own_entry = jnp.take(holders, position)
    narrow = copies.shape[1]
    unit_cols = narrow // 8
    wide_cols = 7 * unit_cols
    scaling = 1.0 / math.sqrt(copies.shape[0])
    gate_pre = jnp.dot(inputs, copies, preferred_element_type=jnp.float32) * scaling
    logistic = jax.nn.sigmoid(gate_pre)
    gate_grad = (
        upstream.astype(jnp.float32)
        * up_act.astype(jnp.float32)
        * logistic
        * (1.0 + gate_pre * (1.0 - logistic))
    ).astype(jnp.bfloat16)
    tokens = gate_grad.shape[0]
    pooled = gathered_copies(gate_grad[:, wide_cols:], "tp", 1)
    pooled = pooled.reshape(tokens, tp_count, unit_cols)
    wanted = position * 7 + jnp.arange(7, dtype=jnp.int32)
    owners = jnp.argmax(holders[None, :] == wanted[:, None], axis=1)
    rebuilt = jnp.take(pooled, owners, axis=1).reshape(tokens, wide_cols)
    block_grad = jnp.where(own_entry == -2, rebuilt, gate_grad[:, :wide_cols])
    product = lax.dot_general(
        inputs, block_grad, (((0,), (0,)), ((), ())), preferred_element_type=jnp.float32
    )
    gradient = lax.psum_scatter(
        (product * scaling).astype(jnp.bfloat16), "rep", scatter_dimension=0, tiled=True
    ).astype(jnp.float32)
    first_new = beta_one * moment1.astype(jnp.float32) + (1.0 - beta_one) * gradient
    second_new = beta_two * moment2.astype(jnp.float32) + (1.0 - beta_two) * gradient * gradient
    step_size = first_new / bias_one / (jnp.sqrt(second_new / bias_two) + epsilon)
    master_next = master - learn_rate * (step_size + weight_decay * master)
    fresh_copy = master_next.astype(jnp.bfloat16)
    full_block = lax.all_gather(fresh_copy, "rep", axis=0, tiled=True)
    height = full_block.shape[0]
    failed_count = tp_count // 8
    root_list = jnp.nonzero(holders == -2, size=failed_count, fill_value=0)[0].astype(jnp.int32)
    slot_start = jnp.maximum(own_entry, 0) % 7 * unit_cols
    slot_ids = jnp.arange(failed_count, dtype=jnp.int32)
    my_slot = jnp.argmax(root_list == position)
    placing = (own_entry == -2) & (slot_ids == my_slot)
    placed = jnp.where(
        placing[None, :, None],
        full_block.astype(jnp.float32)[:, None, :],
        jnp.zeros((height, failed_count, wide_cols), jnp.float32),
    )
    summed = sum_in_two_steps(
        placed.reshape(height, failed_count * wide_cols).astype(jnp.bfloat16), "tp"
    ).astype(jnp.float32)
    summed = summed.astype(jnp.bfloat16)
    source_slot = jnp.argmax(root_list == jnp.maximum(own_entry, 0) // 7)
    adopted = lax.dynamic_slice_in_dim(summed, source_slot * wide_cols + slot_start, unit_cols, 1)
    adopted = jnp.where(own_entry >= 0, adopted, jnp.zeros_like(adopted))
    copy_next = jnp.concatenate([full_block, adopted], axis=1)
    copy_next = jnp.where(own_entry == -2, jnp.zeros_like(copy_next), copy_next)
    return (master_next, first_new.astype(jnp.bfloat16), second_new.astype(jnp.bfloat16), copy_next)


def solution(mesh):
    placed = (
        P(("rep", "tp"), None),
        P("rep", None),
        P("rep", None),
        P("rep", "tp"),
        P("rep", "tp"),
        P("rep", "tp"),
        P("rep", "tp"),
        P("rep", "tp"),
        P("rep", "tp"),
    )
    return jax.shard_map(
        on_device,
        mesh=mesh,
        in_specs=placed,
        out_specs=(P("rep", "tp"), P("rep", "tp"), P("rep", "tp"), P("rep", "tp")),
        check_vma=False,
    )
```

profile of v0, /device:TPU:1, one launch (start us, length us, event | category | flops | bytes accessed | tf_op | source)
XLA Modules:
  0.0 611.0 jit_solution(9419785542743542625)
XLA Ops:
  7.2 0.0 all-gather.5.cloned.1.call-start
  7.2 0.7 all-gather.5.cloned.1.call-update
  7.9 0.7 reduce.47
  8.6 0.7 fusion.9
  9.3 95.7 %all-gather.5.cloned.1.call-done = bf16[1536,4096]{1,0:T(8,128)(2,1)} async-done(((bf16[96,4096]{1,0:T(8,128)(2,1)}), bf16[1536,4096]{1,0:T(8,128)(2,1)}) %all-gather.5.cloned.1.call-update) | async-done | bytes 12582928 | tf_op jit(solution)/shard_map/all_gather | solution.py:54
  105.1 13.7 %gather_fusion = bf16[384,4096]{1,0:T(8,128)(2,1)S(1)} fusion(bf16[1536,4096]{1,0:T(8,128)(2,1)} %all-gather.5.cloned.1.call-done, s32[1024]{0:T(1024)S(1)} %pad_clamp_fusion.1), kind=kCustom, calls=%fused_computation | custom fusion | bytes 6292992 | tf_op jit(solution)/shard_map/jit(_take)/gather | solution.py:55
  118.8 0.0 copy-start
  118.8 8.9 %multiply_convert_fusion.1 = bf16[384,1024]{1,0:T(8,128)(2,1)S(1)} fusion(bf16[384,1024]{1,0:T(8,128)(2,1)} %param.14, bf16[384,1024]{1,0:T(8,128)(2,1)} %param.13, bf16[4096,1024]{1,0:T(8,128)(2,1)} %param.12, bf16[384,4096]{1,0:T(8,128)(2,1)S(1)} %gather_fusion, pred[384]{0:T(512)(128)(4,1)S(1)} %compare_and_fusion.2), kind=kOutput, calls=%fused_computation.12 | convolution fusion | flops 3227910144 | bytes 13894016 | tf_op jit(solution)/shard_map/dot_general | solution.py:62
  127.7 0.0 copy-done
  127.7 0.0 copy-start.3
  127.7 0.8 copy-done.3
  128.5 1.4 broadcast_in_dim.83
  130.0 0.0 copy-start.5
  130.0 3.9 all-to-all-start
  133.9 0.2 reduce-scatter.3.cloned.1.call-start
  134.1 0.0 copy-done.5
  134.1 0.6 constant_dynamic-slice_fusion
  135.4 0.7 iota_reduce_fusion
  136.1 0.1 broadcast_bitcast_fusion
  136.2 20.6 %all-to-all-done = bf16[16,384,128]{2,1,0:T(8,128)(2,1)S(1)} async-done(((bf16[16,384,128]{2,1,0:T(8,128)(2,1)}), bf16[16,384,128]{2,1,0:T(8,128)(2,1)S(1)}, u32[]{:S(2)}, u32[]{:S(2)}) %all-to-all-start) | async-done | bytes 1572896 | tf_op jit(solution)/shard_map/all_to_all | solution.py:18
  156.8 0.0 copy-start.4
  156.8 0.7 gather_fusion.1
  157.5 0.4 copy.17
  157.8 0.4 copy.18
  158.2 0.0 copy-done.4
  158.2 8.6 %multiply_convert_fusion = bf16[4096,896]{1,0:T(8,128)(2,1)} fusion(bf16[384,4096]{1,0:T(8,128)(2,1)} %copy-done, pred[384]{0:T(512)(128)(4,1)S(1)} %compare_and_fusion.2, bf16[384,1024]{1,0:T(8,128)(2,1)S(1)} %copy-done.4, bf16[384,896]{1,0:T(8,128)(2,1)S(1)} %copy.18, pred[896]{0:T(1024)(128)(4,1)S(1)} %broadcast_bitcast_fusion, pred[]{:T(512)} %bitcast.3), kind=kOutput, calls=%fused_computation.4 | convolution fusion | flops 2828173312 | bytes 11863553 | tf_op jit(solution)/shard_map/dot_general | solution.py:77
  166.8 0.0 copy-start.1
  166.8 0.0 copy-start.2
  166.8 0.0 reduce-scatter.3.cloned.1.call-update
  166.8 0.0 all-gather.7.cloned.1.call-start
  166.9 81.4 %reduce-scatter.3.cloned.1.call-done = bf16[512,896]{1,0:T(8,128)(2,1)} async-done(((bf16[4096,896]{1,0:T(8,128)(2,1)}), bf16[512,896]{1,0:T(8,128)(2,1)}) %reduce-scatter.3.cloned.1.call-update) | async-done | bytes 917520 | tf_op jit(solution)/shard_map/reduce_scatter | solution.py:80
  248.3 0.0 copy-done.1
  248.3 0.0 copy-done.2
  248.3 5.7 fusion.17
  254.0 0.0 all-gather.7.cloned.1.call-update
  254.0 0.0 reduce-scatter.5.cloned.1.call-start
  254.1 0.1 copy.19
  254.2 0.1 fusion.8
  254.3 0.7 scatter_custom_fusion
  255.0 0.2 reduce-window.15
  255.2 0.7 fusion.10
  255.9 1.4 compare_reduce_fusion.1
  257.3 0.6 compare_and_fusion
  257.9 0.1 broadcast_in_dim.88
  258.0 77.0 %all-gather.7.cloned.1.call-done = bf16[4096,896]{1,0:T(8,128)(2,1)} async-done(((bf16[512,896]{1,0:T(8,128)(2,1)}), bf16[4096,896]{1,0:T(8,128)(2,1)}) %all-gather.7.cloned.1.call-update) | async-done | bytes 7340048 | tf_op jit(solution)/shard_map/all_gather | solution.py:88
  335.0 10.4 %broadcast_in_dim.91 = bf16[4096,2,896]{2,1,0:T(2,128)(2,1)} broadcast(bf16[4096,896]{1,0:T(8,128)(2,1)} %all-gather.7.cloned.1.call-done), dimensions={0,2} | broadcast | bytes 22020096 | tf_op jit(solution)/shard_map/jit(_where)/broadcast_in_dim | solution.py:96
  345.4 10.0 %copy.20 = bf16[512,8,2,896]{3,1,2,0:T(8,128)(2,1)S(1)} copy(bf16[512,8,2,896]{3,2,1,0:T(2,128)(2,1)} %bitcast.29) | data formatting | bytes 29360128
  355.5 7.2 %select_convert_fusion = bf16[4096,1792]{1,0:T(8,128)(2,1)} fusion(bf16[4096,1792]{1,0:T(8,128)(2,1)S(1)} %bitcast.28, pred[1792]{0:T(1024)(128)(4,1)S(1)} %broadcast_in_dim.89), kind=kLoop, calls=%fused_computation.3 | loop fusion | flops 7340032 | bytes 29361920 | tf_op jit(solution)/shard_map/convert_element_type | solution.py:102
  362.7 0.0 reduce-scatter.5.cloned.1.call-update
  362.7 0.0 all-gather.9.cloned.1.call-start
  362.8 130.8 %reduce-scatter.5.cloned.1.call-done = bf16[256,1792]{1,0:T(8,128)(2,1)} async-done(((bf16[4096,1792]{1,0:T(8,128)(2,1)}), bf16[256,1792]{1,0:T(8,128)(2,1)}) %reduce-scatter.5.cloned.1.call-update) | async-done | bytes 917520 | tf_op jit(solution)/shard_map/reduce_scatter | solution.py:41
  493.6 0.0 all-gather.9.cloned.1.call-update
  493.6 1.3 compare_reduce_fusion
  495.5 100.2 %all-gather.9.cloned.1.call-done = bf16[4096,1792]{1,0:T(8,128)(2,1)} async-done(((bf16[256,1792]{1,0:T(8,128)(2,1)}), bf16[4096,1792]{1,0:T(8,128)(2,1)}) %all-gather.9.cloned.1.call-update) | async-done | bytes 14680080 | tf_op jit(solution)/shard_map/all_gather | solution.py:44
  595.7 1.4 dynamic-slice_select_fusion
  597.1 7.3 %maximum_select_fusion = bf16[4096,1024]{1,0:T(8,128)(2,1)} fusion(bf16[4096,128]{1,0:T(8,128)(2,1)S(1)} %dynamic-slice_select_fusion, bf16[4096,896]{1,0:T(8,128)(2,1)} %all-gather.7.cloned.1.call-done, pred[]{:T(512)} %bitcast.3), kind=kLoop, calls=%fused_computation.5 | loop fusion | flops 20971520 | bytes 16777216 | tf_op jit(solution)/shard_map/jit(_where)/select_n | solution.py:109
  (11 shorter events, 0.1 us)
Async XLA Ops:
  7.2 97.9 %all-gather.5.cloned.1.call-start = ((), (), s32[]{:S(2)}) async-start(), calls=%async_computation.3 | async-start | bytes 13369344 | tf_op jit(solution)/shard_map/all_gather | solution.py:54
  118.8 8.9 %copy-start = (bf16[384,4096]{1,0:T(8,128)(2,1)}, bf16[384,4096]{1,0:T(8,128)(2,1)S(1)}, u32[]{:S(2)}) copy-start(bf16[384,4096]{1,0:T(8,128)(2,1)S(1)} %gather_fusion) | copy-start | bytes 9437188
  127.7 0.9 copy-start.3
  130.0 4.1 copy-start.5
  130.0 26.8 %all-to-all-start = ((bf16[16,384,128]{2,1,0:T(8,128)(2,1)}), bf16[16,384,128]{2,1,0:T(8,128)(2,1)S(1)}, u32[]{:S(2)}, u32[]{:S(2)}) async-start(bf16[16,384,128]{2,1,0:T(8,128)(2,1)} %broadcast_in_dim.83), calls=%async_computation | async-start | bytes 3145728 | tf_op jit(solution)/shard_map/all_to_all | solution.py:18
  133.9 114.4 %reduce-scatter.3.cloned.1.call-start = ((), (), s32[]{:S(2)}) async-start(), calls=%async_computation.4 | async-start | bytes 8257536 | tf_op jit(solution)/shard_map/reduce_scatter | solution.py:80
  156.8 1.4 copy-start.4
  166.8 81.5 %copy-start.1 = (f32[512,896]{1,0:T(8,128)S(1)}, f32[512,896]{1,0:T(8,128)}, u32[]{:S(2)}) copy-start(f32[512,896]{1,0:T(8,128)} %param.15) | copy-start | bytes 5505028
  166.8 81.5 %copy-start.2 = (bf16[512,896]{1,0:T(8,128)(2,1)S(1)}, bf16[512,896]{1,0:T(8,128)(2,1)}, u32[]{:S(2)}) copy-start(bf16[512,896]{1,0:T(8,128)(2,1)} %param.17) | copy-start | bytes 2752516
  166.8 168.2 %all-gather.7.cloned.1.call-start = ((), (), s32[]{:S(2)}) async-start(), calls=%async_computation.5 | async-start | bytes 8257536 | tf_op jit(solution)/shard_map/all_gather | solution.py:88
  254.0 239.5 %reduce-scatter.5.cloned.1.call-start = ((), (), s32[]{:S(2)}) async-start(), calls=%async_computation.6 | async-start | bytes 15597568 | tf_op jit(solution)/shard_map/reduce_scatter | solution.py:41
  362.7 233.0 %all-gather.9.cloned.1.call-start = ((), (), s32[]{:S(2)}) async-start(), calls=%async_computation.7 | async-start | bytes 15597568 | tf_op jit(solution)/shard_map/all_gather | solution.py:44
Sparse Core Ops, SparseCore 0:
  10.4 94.6 all-gather.4
  166.9 81.2 reduce-scatter.2
  254.2 80.8 all-gather.6
  362.9 130.6 reduce-scatter.4
  496.1 99.5 all-gather.8
where the time goes:
time: 612 us; the launch traced here: 611 us
  waiting for transfers between devices  506 us (83%)
  local copies, waits for them, and re-layouts  38.7 us (6%)
  other arithmetic  29 us (5%)
  matrix products  17.5 us (3%)
  between operations  15.2 us (2%)
    reduce_scatter x1, waiting for transfers between devices, sum_in_two_steps(): lax.psum_scatter(rows_for(lines, lax.axis_size(axis)), axis, scatter_dime...  131 us
    all_gather x1, waiting for transfers between devices, sum_in_two_steps(): whole = lax.all_gather(own, axis).reshape(-1, *lines.shape[1:])  100 us
    all_gather x1, waiting for transfers between devices, on_device(): whole_batch = lax.all_gather(batch_rows, 'tp', axis=0, tiled=True)  95.7 us
    reduce_scatter x1, waiting for transfers between devices, on_device(): lax.psum_scatter((product * scaling).astype(jnp.bfloat16), 'rep', scatter...  81.4 us
    all_gather x1, waiting for transfers between devices, on_device(): full_block = lax.all_gather(fresh_copy, 'rep', axis=0, tiled=True)  77 us
    all_to_all x1, waiting for transfers between devices, from_everyone(): return lax.all_to_all(copies, axis, split_axis=0, concat_axis=0, tiled=True)  20.6 us
    gather x1, local copies, waits for them, and re-layouts, on_device(): inputs = jnp.take(whole_batch, chosen, axis=0)  13.7 us
  transfers between devices with their start and end apart: 6, of which 6 were waited for; matrix products, arithmetic and copies ran while one was open for 1% of the time, Pallas kernels for 0%

commit v1 on v0

--- a/solution.py
+++ b/solution.py
@@ -51,7 +51,10 @@
     tp_count = lax.axis_size("tp")
     position = lax.axis_index("tp")
     chosen = token_slots[0]
-    whole_batch = lax.all_gather(batch_rows, "tp", axis=0, tiled=True)
+    size = lax.axis_size("tp")
+    tiles = jnp.stack([batch_rows for _ in range(size)])
+    tiles = lax.all_to_all(tiles, "tp", split_axis=0, concat_axis=0)
+    whole_batch = jnp.concatenate(tiles, axis=0)
     inputs = jnp.take(whole_batch, chosen, axis=0)
     holders = holder_map[0]
     own_entry = jnp.take(holders, position)

time: 612 us -> 735 us (1.20)
  waiting for transfers between devices: 506 us -> 610 us
  starting transfers between devices: 4.26 us -> 18.1 us
    all_to_all x0 -> x1, waiting for transfers between devices: none -> 200 us  [on_device(): tiles = lax.all_to_all(tiles, 'tp', split_axis=0, concat_axis=0)]
    all_gather x1 -> x0, waiting for transfers between devices: 95.7 us -> none  [on_device(): whole_batch = lax.all_gather(batch_rows, 'tp', axis=0, tiled=True)]
    all_to_all x0 -> x1, starting transfers between devices: none -> 9.43 us  [on_device(): tiles = lax.all_to_all(tiles, 'tp', split_axis=0, concat_axis=0)]
where the time goes in v1:
time: 735 us
  waiting for transfers between devices  610 us (83%)
  local copies, waits for them, and re-layouts  45.9 us (6%)
  other arithmetic  27.6 us (4%)
  starting transfers between devices  18.1 us (2%)
  matrix products  17.5 us (2%)
  between operations  15.2 us (2%)
    all_to_all x1, waiting for transfers between devices, on_device(): tiles = lax.all_to_all(tiles, 'tp', split_axis=0, concat_axis=0)  200 us
    reduce_scatter x1, waiting for transfers between devices, sum_in_two_steps(): lax.psum_scatter(rows_for(lines, lax.axis_size(axis)), axis, scatter_dime...  131 us
    all_gather x1, waiting for transfers between devices, sum_in_two_steps(): whole = lax.all_gather(own, axis).reshape(-1, *lines.shape[1:])  100 us
    reduce_scatter x1, waiting for transfers between devices, on_device(): lax.psum_scatter((product * scaling).astype(jnp.bfloat16), 'rep', scatter...  81.7 us
    all_gather x1, waiting for transfers between devices, on_device(): full_block = lax.all_gather(fresh_copy, 'rep', axis=0, tiled=True)  76.9 us
    all_to_all x1, waiting for transfers between devices, from_everyone(): return lax.all_to_all(copies, axis, split_axis=0, concat_axis=0, tiled=True)  20.5 us
  transfers between devices with their start and end apart: 6, of which 6 were waited for; matrix products, arithmetic and copies ran while one was open for 1% of the time, Pallas kernels for 0%

profile of v1, /device:TPU:1, one launch (start us, length us, event | category | flops | bytes accessed | tf_op | source)
XLA Modules:
  0.0 734.6 jit_solution(12424222608031279006)
XLA Ops:
  7.2 7.2 stack.2
  14.4 0.0 copy-start.5
  14.4 9.4 %all-to-all-start = ((bf16[16,96,4096]{2,1,0:T(8,128)(2,1)}), bf16[16,96,4096]{2,1,0:T(8,128)(2,1)}, u32[]{:S(2)}, u32[]{:S(2)}) async-start(bf16[16,96,4096]{2,1,0:T(8,128)(2,1)} %stack.2), calls=%async_computation | async-start | bytes 25165824 | tf_op jit(solution)/shard_map/all_to_all | solution.py:56
  23.8 0.0 copy-done.5
  23.9 200.1 %all-to-all-done = bf16[16,96,4096]{2,1,0:T(8,128)(2,1)} async-done(((bf16[16,96,4096]{2,1,0:T(8,128)(2,1)}), bf16[16,96,4096]{2,1,0:T(8,128)(2,1)}, u32[]{:S(2)}, u32[]{:S(2)}) %all-to-all-start) | async-done | bytes 12582944 | tf_op jit(solution)/shard_map/all_to_all | solution.py:56
  224.0 13.7 %gather_fusion = bf16[384,4096]{1,0:T(8,128)(2,1)S(1)} fusion(bf16[1536,4096]{1,0:T(8,128)(2,1)} %bitcast, s32[1024]{0:T(1024)S(1)} %pad_clamp_fusion.1), kind=kCustom, calls=%fused_computation | custom fusion | bytes 6292992 | tf_op jit(solution)/shard_map/jit(_take)/gather | solution.py:58
  237.7 0.0 copy-start
  237.7 8.9 %multiply_convert_fusion.1 = bf16[384,1024]{1,0:T(8,128)(2,1)S(1)} fusion(bf16[384,1024]{1,0:T(8,128)(2,1)} %param.14, bf16[384,1024]{1,0:T(8,128)(2,1)} %param.13, bf16[4096,1024]{1,0:T(8,128)(2,1)} %param.12, bf16[384,4096]{1,0:T(8,128)(2,1)S(1)} %gather_fusion, pred[384]{0:T(512)(128)(4,1)S(1)} %compare_and_fusion.2), kind=kOutput, calls=%fused_computation.12 | convolution fusion | flops 3227910144 | bytes 13894016 | tf_op jit(solution)/shard_map/dot_general | solution.py:65
  246.6 0.0 copy-done
  246.6 0.0 copy-start.3
  246.6 0.8 copy-done.3
  247.5 1.4 broadcast_in_dim.83
  248.9 0.0 copy-start.6
  248.9 8.3 %all-to-all-start.1 = ((bf16[16,384,128]{2,1,0:T(8,128)(2,1)}), bf16[16,384,128]{2,1,0:T(8,128)(2,1)S(1)}, u32[]{:S(2)}, u32[]{:S(2)}) async-start(bf16[16,384,128]{2,1,0:T(8,128)(2,1)} %broadcast_in_dim.83), calls=%async_computation.1 | async-start | bytes 3145728 | tf_op jit(solution)/shard_map/all_to_all | solution.py:18
  257.2 0.2 reduce-scatter.3.cloned.1.call-start
  257.5 0.0 copy-done.6
  257.5 0.6 constant_dynamic-slice_fusion
  258.7 0.7 iota_reduce_fusion
  259.4 0.1 broadcast_bitcast_fusion
  259.5 20.5 %all-to-all-done.1 = bf16[16,384,128]{2,1,0:T(8,128)(2,1)S(1)} async-done(((bf16[16,384,128]{2,1,0:T(8,128)(2,1)}), bf16[16,384,128]{2,1,0:T(8,128)(2,1)S(1)}, u32[]{:S(2)}, u32[]{:S(2)}) %all-to-all-start.1) | async-done | bytes 1572896 | tf_op jit(solution)/shard_map/all_to_all | solution.py:18
  280.1 0.0 copy-start.4
  280.1 0.7 gather_fusion.1
  280.7 0.4 copy.17
  281.1 0.4 copy.18
  281.5 0.0 copy-done.4
  281.5 8.6 %multiply_convert_fusion = bf16[4096,896]{1,0:T(8,128)(2,1)} fusion(bf16[384,4096]{1,0:T(8,128)(2,1)} %copy-done, pred[384]{0:T(512)(128)(4,1)S(1)} %compare_and_fusion.2, bf16[384,1024]{1,0:T(8,128)(2,1)S(1)} %copy-done.4, bf16[384,896]{1,0:T(8,128)(2,1)S(1)} %copy.18, pred[896]{0:T(1024)(128)(4,1)S(1)} %broadcast_bitcast_fusion, pred[]{:T(512)} %bitcast.4), kind=kOutput, calls=%fused_computation.4 | convolution fusion | flops 2828173312 | bytes 11863553 | tf_op jit(solution)/shard_map/dot_general | solution.py:80
  290.1 0.0 copy-start.1
  290.1 0.0 copy-start.2
  290.1 0.0 reduce-scatter.3.cloned.1.call-update
  290.1 0.0 all-gather.4.cloned.1.call-start
  290.1 81.7 %reduce-scatter.3.cloned.1.call-done = bf16[512,896]{1,0:T(8,128)(2,1)} async-done(((bf16[4096,896]{1,0:T(8,128)(2,1)}), bf16[512,896]{1,0:T(8,128)(2,1)}) %reduce-scatter.3.cloned.1.call-update) | async-done | bytes 917520 | tf_op jit(solution)/shard_map/reduce_scatter | solution.py:83
  371.9 0.0 copy-done.1
  371.9 0.0 copy-done.2
  371.9 5.7 fusion.17
  377.6 0.0 all-gather.4.cloned.1.call-update
  377.6 0.0 reduce-scatter.5.cloned.1.call-start
  377.7 0.1 copy.19
  377.8 0.1 fusion.8
  377.9 0.7 scatter_custom_fusion
  378.6 0.2 reduce-window.15
  378.8 0.7 fusion.10
  379.5 1.4 compare_reduce_fusion.1
  380.9 0.6 compare_and_fusion
  381.5 0.1 broadcast_in_dim.88
  381.6 76.9 %all-gather.4.cloned.1.call-done = bf16[4096,896]{1,0:T(8,128)(2,1)} async-done(((bf16[512,896]{1,0:T(8,128)(2,1)}), bf16[4096,896]{1,0:T(8,128)(2,1)}) %all-gather.4.cloned.1.call-update) | async-done | bytes 7340048 | tf_op jit(solution)/shard_map/all_gather | solution.py:91
  458.6 10.4 %broadcast_in_dim.91 = bf16[4096,2,896]{2,1,0:T(2,128)(2,1)} broadcast(bf16[4096,896]{1,0:T(8,128)(2,1)} %all-gather.4.cloned.1.call-done), dimensions={0,2} | broadcast | bytes 22020096 | tf_op jit(solution)/shard_map/jit(_where)/broadcast_in_dim | solution.py:99
  469.0 10.0 %copy.20 = bf16[512,8,2,896]{3,1,2,0:T(8,128)(2,1)S(1)} copy(bf16[512,8,2,896]{3,2,1,0:T(2,128)(2,1)} %bitcast.30) | data formatting | bytes 29360128
  479.0 7.2 select_convert_fusion
  486.3 0.0 reduce-scatter.5.cloned.1.call-update
  486.3 0.0 all-gather.6.cloned.1.call-start
  486.3 130.8 %reduce-scatter.5.cloned.1.call-done = bf16[256,1792]{1,0:T(8,128)(2,1)} async-done(((bf16[4096,1792]{1,0:T(8,128)(2,1)}), bf16[256,1792]{1,0:T(8,128)(2,1)}) %reduce-scatter.5.cloned.1.call-update) | async-done | bytes 917520 | tf_op jit(solution)/shard_map/reduce_scatter | solution.py:41
  617.1 0.0 all-gather.6.cloned.1.call-update
  617.2 1.3 compare_reduce_fusion
  619.1 100.2 %all-gather.6.cloned.1.call-done = bf16[4096,1792]{1,0:T(8,128)(2,1)} async-done(((bf16[256,1792]{1,0:T(8,128)(2,1)}), bf16[4096,1792]{1,0:T(8,128)(2,1)}) %all-gather.6.cloned.1.call-update) | async-done | bytes 14680080 | tf_op jit(solution)/shard_map/all_gather | solution.py:44
  719.2 1.4 dynamic-slice_select_fusion
  720.7 7.3 maximum_select_fusion
  (13 shorter events, 0.2 us)
Async XLA Ops:
  14.4 9.4 %copy-start.5 = (s32[1,384]{1,0:T(1,128)S(1)}, s32[1,384]{1,0:T(1,128)}, u32[]{:S(2)}) copy-start(s32[1,384]{1,0:T(1,128)} %param.10) | copy-start | bytes 4612
  14.4 209.6 %all-to-all-start = ((bf16[16,96,4096]{2,1,0:T(8,128)(2,1)}), bf16[16,96,4096]{2,1,0:T(8,128)(2,1)}, u32[]{:S(2)}, u32[]{:S(2)}) async-start(bf16[16,96,4096]{2,1,0:T(8,128)(2,1)} %stack.2), calls=%async_computation | async-start | bytes 25165824 | tf_op jit(solution)/shard_map/all_to_all | solution.py:56
  237.7 8.9 %copy-start = (bf16[384,4096]{1,0:T(8,128)(2,1)}, bf16[384,4096]{1,0:T(8,128)(2,1)S(1)}, u32[]{:S(2)}) copy-start(bf16[384,4096]{1,0:T(8,128)(2,1)S(1)} %gather_fusion) | copy-start | bytes 9437188
  246.6 0.9 copy-start.3
  248.9 8.6 %copy-start.6 = (s32[1,16]{1,0:T(1,128)S(1)}, s32[1,16]{1,0:T(1,128)}, u32[]{:S(2)}) copy-start(s32[1,16]{1,0:T(1,128)} %param.11) | copy-start | bytes 196
  248.9 31.1 %all-to-all-start.1 = ((bf16[16,384,128]{2,1,0:T(8,128)(2,1)}), bf16[16,384,128]{2,1,0:T(8,128)(2,1)S(1)}, u32[]{:S(2)}, u32[]{:S(2)}) async-start(bf16[16,384,128]{2,1,0:T(8,128)(2,1)} %broadcast_in_dim.83), calls=%async_computation.1 | async-start | bytes 3145728 | tf_op jit(solution)/shard_map/all_to_all | solution.py:18
  257.2 114.6 %reduce-scatter.3.cloned.1.call-start = ((), (), s32[]{:S(2)}) async-start(), calls=%async_computation.4 | async-start | bytes 8257536 | tf_op jit(solution)/shard_map/reduce_scatter | solution.py:83
  280.1 1.4 copy-start.4
  290.1 81.8 %copy-start.1 = (f32[512,896]{1,0:T(8,128)S(1)}, f32[512,896]{1,0:T(8,128)}, u32[]{:S(2)}) copy-start(f32[512,896]{1,0:T(8,128)} %param.15) | copy-start | bytes 5505028
  290.1 81.8 %copy-start.2 = (bf16[512,896]{1,0:T(8,128)(2,1)S(1)}, bf16[512,896]{1,0:T(8,128)(2,1)}, u32[]{:S(2)}) copy-start(bf16[512,896]{1,0:T(8,128)(2,1)} %param.17) | copy-start | bytes 2752516
  290.1 168.5 %all-gather.4.cloned.1.call-start = ((), (), s32[]{:S(2)}) async-start(), calls=%async_computation.5 | async-start | bytes 8257536 | tf_op jit(solution)/shard_map/all_gather | solution.py:91
  377.6 239.5 %reduce-scatter.5.cloned.1.call-start = ((), (), s32[]{:S(2)}) async-start(), calls=%async_computation.6 | async-start | bytes 15597568 | tf_op jit(solution)/shard_map/reduce_scatter | solution.py:41
  486.3 233.0 %all-gather.6.cloned.1.call-start = ((), (), s32[]{:S(2)}) async-start(), calls=%async_computation.7 | async-start | bytes 15597568 | tf_op jit(solution)/shard_map/all_gather | solution.py:44
Sparse Core Ops, SparseCore 0:
  290.2 81.5 reduce-scatter.2
  377.7 80.7 all-gather.3
  486.4 130.6 reduce-scatter.4
  619.7 99.5 all-gather.5
